TPU v7x, 256 devices: a whole 4x4x8 slice. The times are simulated.
256 devices in a mesh: rows: 128 (over x, z, y), cols: 2 (over core).
Axes of the slice: x: 4, y: 4, z: 8, core: 2. Of those that a mesh axis runs over, the one named last changes fastest.
Arguments:
- embeddings: bfloat16 [262144, 384], P('rows')
- test_matrix: bfloat16 [262144, 64], P('rows'), may hold values from -6 to 6
- pair_list: int32 [1024, 2], P(('rows', 'cols')), may hold values from -1 to 255, as said below
Outputs:
- orthonormal_basis: float32 [262144, 64], P(('rows', 'cols'))
- upper_factor: float32 [64, 64], replicated
Inputs may be any that keep to these rules, and one draw needn't show every extreme that they name: `pair_list`: device (r, c) holds 4 entries. Its live entries come first: pairs (i, j) with r * 2 <= i < (r + 1) * 2 and i <= j < min((r + 3) * 2, 256); each pair appears at most once over all devices; its other entries are -1 in both places. The device with c = 0 holds at least one live pair, the two devices of one r hold at most 4 together, and device (0, 0) holds exactly 4.
All inputs are finite; a program needn't handle non-finite values.
Results may differ from a plain program's by a relative error of at most 0.0053.
Values may be sent and summed in bfloat16 or wider, within the bound.
No kernel may reach another device: no remote copies, remote signals or barrier semaphores. Data moves between devices by JAX's collectives and lax.ppermute only.
A program may use at most 64 MiB of HBM per device.

v0:
```python
import jax
import jax.numpy as jnp
from jax import lax
from jax.sharding import PartitionSpec as P

BLK = 1024
SHARPNESS = 6.0
EPSILON = 1e-06


def shifted(value, axis, steps):
    count = lax.axis_size(axis)
    initial, last = (max(0, -steps), min(count, count - steps))
    return lax.ppermute(value, axis, [(source, source + steps) for source in range(initial, last)])


def unit_rows(embeddings):
    widened = embeddings.astype(jnp.float32)
    inverse = lax.rsqrt(jnp.sum(widened * widened, axis=1, keepdims=True) + EPSILON)
    return (widened * inverse).astype(jnp.bfloat16)


def affinity(left_rows, right_rows):
    scores = lax.dot_general(
        left_rows, right_rows, (((1,), (1,)), ((), ())), preferred_element_type=jnp.float32
    )
    return jnp.exp(SHARPNESS * (scores - 1.0)).astype(jnp.bfloat16)


def mirror_product(affinity_tile, vectors):
    return lax.dot_general(
        affinity_tile, vectors, (((0,), (0,)), ((), ())), preferred_element_type=jnp.float32
    )


def block_at(stacked, index):
    return lax.dynamic_index_in_dim(stacked, index, 0, keepdims=False)


def add_block(stacked, index, term):
    return lax.dynamic_update_index_in_dim(stacked, block_at(stacked, index) + term, index, 0)


def count_live(pair_rows):
    return jnp.sum((pair_rows[:, 0] >= 0).astype(jnp.int32))


def orthonormal(sketch_rows, rows_total):
    gram_matrix = lax.dot_general(
        sketch_rows,
        sketch_rows,
        (((0,), (0,)), ((), ())),
        precision=lax.Precision.HIGHEST,
        preferred_element_type=jnp.float32,
    )
    gram_matrix = lax.psum(gram_matrix, ("rows", "cols")) / rows_total
    lower_factor = jnp.linalg.cholesky(gram_matrix)
    solved = lax.linalg.triangular_solve(
        lower_factor, sketch_rows, left_side=False, lower=True, transpose_a=True
    )
    return (solved, lower_factor.T)


def affinity_pass(window_units, own_vectors, my_pairs, base_block):
    blocks_dev = own_vectors.shape[0]
    ahead_vectors = [shifted(own_vectors, "rows", -offset) for offset in (1, 2)]
    window_vectors = jnp.concatenate([own_vectors] + ahead_vectors, axis=0)
    initial = jnp.zeros(window_vectors.shape, jnp.float32)

    def pair_step(slot_index, accumulated):
        entry = my_pairs[slot_index]
        first_block = entry[0] - base_block
        second_block = entry[1] - base_block
        affinity_tile = affinity(
            block_at(window_units, first_block), block_at(window_units, second_block)
        )
        forward = jnp.dot(
            affinity_tile,
            block_at(window_vectors, second_block),
            preferred_element_type=jnp.float32,
        )
        accumulated = add_block(accumulated, first_block, forward)
        mirrored = first_block != second_block

        def add_mirror(current):
            return add_block(
                current,
                second_block,
                mirror_product(affinity_tile, block_at(window_vectors, first_block)),
            )

        return lax.cond(mirrored, add_mirror, lambda unchanged: unchanged, accumulated)

    accumulated = lax.fori_loop(0, count_live(my_pairs), pair_step, initial)
    own_blocks = accumulated[:blocks_dev]
    for offset in (1, 2):
        own_blocks = own_blocks + shifted(
            accumulated[offset * blocks_dev : (offset + 1) * blocks_dev], "rows", offset
        )
    flattened = own_blocks.reshape(-1, own_blocks.shape[2])
    return lax.psum_scatter(flattened, "cols", scatter_dimension=0, tiled=True)


def local(embeddings, test_matrix, pair_list):
    rows_dev = embeddings.shape[0]
    blocks_dev = rows_dev // BLK
    columns = test_matrix.shape[1]
    base_block = lax.axis_index("rows") * blocks_dev
    rows_total = rows_dev * lax.axis_size("rows")
    normed = unit_rows(embeddings).reshape(blocks_dev, BLK, embeddings.shape[1])
    ahead_units = [shifted(normed, "rows", -offset) for offset in (1, 2)]
    window_units = jnp.concatenate([normed] + ahead_units, axis=0)
    sketch_rows = affinity_pass(
        window_units, test_matrix.reshape(blocks_dev, BLK, columns), pair_list, base_block
    )
    panel_rows, _ = orthonormal(sketch_rows, rows_total)
    panel_whole = lax.all_gather(panel_rows.astype(jnp.bfloat16), "cols", axis=0, tiled=True)
    image_rows = affinity_pass(
        window_units, panel_whole.reshape(blocks_dev, BLK, columns), pair_list, base_block
    )
    return orthonormal(image_rows, rows_total)


def solution(mesh):
    in_specs = (P("rows", None), P("rows", None), P(("rows", "cols"), None))
    out_specs = (P(("rows", "cols"), None), P())
    return jax.shard_map(local, mesh=mesh, in_specs=in_specs, out_specs=out_specs, check_vma=False)
```

profile of v0, /device:TPU:1, one launch (start us, length us, event | category | flops | bytes accessed | tf_op | source)
XLA Modules:
  0.0 547.8 jit_solution(13680197383918252103)
XLA Ops:
  7.2 1.9 fusion.32
  9.5 1.3 collective-permute-start
  15.7 85.9 %collective-permute-done.2 = bf16[2,1024,64]{2,1,0:T(8,128)(2,1)S(1)} collective-permute-done((bf16[2,1024,64]{2,1,0:T(8,128)(2,1)S(1)}, bf16[2,1024,64]{2,1,0:T(8,128)(2,1)S(1)}, u32[]{:S(2)}, u32[]{:S(2)}) %collective-permute-start.2) | collective-permute-done | bytes 262176 | tf_op jit(solution)/shard_map/ppermute | solution.py:14
  101.6 1.5 pad_maximum_fusion.1
  103.1 3.8 pad_maximum_fusion
  106.9 1.3 broadcast.76.clone
  108.9 1.3 fusion.48
  110.2 6.4 %collective-permute-start.4 = (f32[2,1024,64]{1,2,0:T(8,128)S(1)}, f32[2,1024,64]{1,2,0:T(8,128)S(1)}, u32[]{:S(2)}, u32[]{:S(2)}) collective-permute-start(f32[2,1024,64]{1,2,0:T(8,128)S(1)} %get-tuple-element.272), channel_id=1, source_target_pairs={{0,2},{2,4},{4,6},{6,8},{8,10},{10,12},{12,14},{14,16},{16,18},{18... | collective-permute-start | bytes 1572872 | tf_op jit(solution)/shard_map/ppermute | solution.py:14
  116.6 72.9 %collective-permute-start.5 = (f32[2,1024,64]{1,2,0:T(8,128)S(1)}, f32[2,1024,64]{1,2,0:T(8,128)S(1)}, u32[]{:S(2)}, u32[]{:S(2)}) collective-permute-start(f32[2,1024,64]{1,2,0:T(8,128)S(1)} %get-tuple-element.273), channel_id=1, source_target_pairs={{0,4},{2,6},{4,8},{6,10},{8,12},{10,14},{12,16},{14,18},{16,20},{1... | collective-permute-start | bytes 1572872 | tf_op jit(solution)/shard_map/ppermute | solution.py:14
  189.5 6.1 %collective-permute-done.5 = f32[2,1024,64]{1,2,0:T(8,128)S(1)} collective-permute-done((f32[2,1024,64]{1,2,0:T(8,128)S(1)}, f32[2,1024,64]{1,2,0:T(8,128)S(1)}, u32[]{:S(2)}, u32[]{:S(2)}) %collective-permute-start.5) | collective-permute-done | bytes 524320 | tf_op jit(solution)/shard_map/ppermute | solution.py:14
  197.7 36.3 %reduce-scatter.3.cloned.1.call-done = f32[1024,64]{0,1:T(8,128)} async-done(((f32[2048,64]{0,1:T(8,128)}), f32[1024,64]{0,1:T(8,128)}) %reduce-scatter.3.cloned.1.call-update) | async-done | bytes 262160 | tf_op jit(solution)/shard_map/reduce_scatter | solution.py:101
  234.0 1.4 fusion.49
  235.5 77.5 %psum.14 = f32[64,64]{0,1:T(8,128)S(1)} all-reduce(f32[64,64]{0,1:T(8,128)S(1)} %fusion.49), channel_id=1, replica_groups=mesh['rows'=128,'cols'=2] {'rows','cols'}, use_global_device_ids=true, to_apply=%region_7.8 | all-reduce | flops 4096 | bytes 32768 | tf_op jit(solution)/shard_map/psum | solution.py:56
  313.1 5.8 %cholesky.44 = f32[64,64]{1,0:T(8,128)S(1)} custom-call(f32[64,64]{1,0:T(8,128)S(1)} %fusion.39), custom_call_target="Cholesky" | custom-call | tf_op jit(solution)/shard_map/jit(cholesky)/cholesky | solution.py:57
  320.3 4.9 custom-call.6
  325.2 1.4 fusion.34
  326.6 2.5 all_gather.3
  329.4 1.3 collective-permute-start.6
  330.7 1.3 collective-permute-start.7
  332.0 22.3 %collective-permute-done.6 = bf16[2,1024,64]{2,1,0:T(8,128)(2,1)S(1)} collective-permute-done((bf16[2,1024,64]{2,1,0:T(8,128)(2,1)S(1)}, bf16[2,1024,64]{2,1,0:T(8,128)(2,1)S(1)}, u32[]{:S(2)}, u32[]{:S(2)}) %collective-permute-start.6) | collective-permute-done | bytes 262176 | tf_op jit(solution)/shard_map/ppermute | solution.py:14
  354.2 1.5 pad_maximum_fusion.2
  355.8 1.3 broadcast.76
  357.7 1.3 fusion.47
  359.1 3.7 collective-permute-start.8
  362.7 45.1 %collective-permute-start.9 = (f32[2,1024,64]{1,2,0:T(8,128)S(1)}, f32[2,1024,64]{1,2,0:T(8,128)S(1)}, u32[]{:S(2)}, u32[]{:S(2)}) collective-permute-start(f32[2,1024,64]{1,2,0:T(8,128)S(1)} %get-tuple-element.271), channel_id=1, source_target_pairs={{0,4},{2,6},{4,8},{6,10},{8,12},{10,14},{12,16},{14,18},{16,20},{1... | collective-permute-start | bytes 1572872 | tf_op jit(solution)/shard_map/ppermute | solution.py:14
  407.8 11.5 %collective-permute-done.9 = f32[2,1024,64]{1,2,0:T(8,128)S(1)} collective-permute-done((f32[2,1024,64]{1,2,0:T(8,128)S(1)}, f32[2,1024,64]{1,2,0:T(8,128)S(1)}, u32[]{:S(2)}, u32[]{:S(2)}) %collective-permute-start.9) | collective-permute-done | bytes 524320 | tf_op jit(solution)/shard_map/ppermute | solution.py:14
  421.3 25.8 %reduce-scatter.5.cloned.1.call-done = f32[1024,64]{0,1:T(8,128)} async-done(((f32[2048,64]{0,1:T(8,128)}), f32[1024,64]{0,1:T(8,128)}) %reduce-scatter.5.cloned.1.call-update) | async-done | bytes 262160 | tf_op jit(solution)/shard_map/reduce_scatter | solution.py:101
  447.1 1.4 fusion.50
  448.4 77.5 %psum.15 = f32[64,64]{0,1:T(8,128)S(1)} all-reduce(f32[64,64]{0,1:T(8,128)S(1)} %fusion.50), channel_id=1, replica_groups=mesh['rows'=128,'cols'=2] {'rows','cols'}, use_global_device_ids=true, to_apply=%region_15.18 | all-reduce | flops 4096 | bytes 32768 | tf_op jit(solution)/shard_map/psum | solution.py:56
  526.1 5.8 %cholesky.55 = f32[64,64]{1,0:T(8,128)S(1)} custom-call(f32[64,64]{1,0:T(8,128)S(1)} %fusion.37), custom_call_target="Cholesky" | custom-call | tf_op jit(solution)/shard_map/jit(cholesky)/cholesky | solution.py:57
  533.3 4.9 custom-call.7
  538.9 2.1 convolution_bitcast_fusion.2
  (43 shorter events, 14.4 us)
Async XLA Ops:
  7.2 2.0 copy-start
  7.2 226.9 %reduce-scatter.3.cloned.1.call-start = ((), (), s32[]{:S(2)}) async-start(), calls=%async_computation.2 | async-start | bytes 786432 | tf_op jit(solution)/shard_map/reduce_scatter | solution.py:101
  9.1 3.0 copy-start.1
  9.2 5.9 %copy-start.2 = (s32[4,2]{0,1:T(2,128)S(1)}, s32[4,2]{0,1:T(2,128)}, u32[]{:S(2)}) copy-start(s32[4,2]{0,1:T(2,128)} %param.16) | copy-start | bytes 100
  9.5 93.6 %collective-permute-start = (bf16[2,1024,384]{2,1,0:T(8,128)(2,1)S(1)}, bf16[2,1024,384]{2,1,0:T(8,128)(2,1)}, u32[]{:S(2)}, u32[]{:S(2)}) collective-permute-start(bf16[2,1024,384]{2,1,0:T(8,128)(2,1)S(1)} %bitcast.145), channel_id=1, source_target_pairs={{2,0},{4,2},{6,4},{8,6},{10,8},{12,10},{14,12},{16,14},{18,16},{20... | collective-permute-start | bytes 4718600 | tf_op jit(solution)/shard_map/ppermute | solution.py:14
  10.8 92.3 %collective-permute-start.1 = (bf16[2,1024,384]{2,1,0:T(8,128)(2,1)S(1)}, bf16[2,1024,384]{2,1,0:T(8,128)(2,1)}, u32[]{:S(2)}, u32[]{:S(2)}) collective-permute-start(bf16[2,1024,384]{2,1,0:T(8,128)(2,1)S(1)} %bitcast.146), channel_id=1, source_target_pairs={{4,0},{6,2},{8,4},{10,6},{12,8},{14,10},{16,12},{18,14},{20,16},{2... | collective-permute-start | bytes 4718600 | tf_op jit(solution)/shard_map/ppermute | solution.py:14
  12.4 89.2 %collective-permute-start.2 = (bf16[2,1024,64]{2,1,0:T(8,128)(2,1)S(1)}, bf16[2,1024,64]{2,1,0:T(8,128)(2,1)S(1)}, u32[]{:S(2)}, u32[]{:S(2)}) collective-permute-start(bf16[2,1024,64]{2,1,0:T(8,128)(2,1)S(1)} %bitcast.150), channel_id=1, source_target_pairs={{2,0},{4,2},{6,4},{8,6},{10,8},{12,10},{14,12},{16,14},{18,16},{20... | collective-permute-start | bytes 786440 | tf_op jit(solution)/shard_map/ppermute | solution.py:14
  13.7 87.9 %collective-permute-start.3 = (bf16[2,1024,64]{2,1,0:T(8,128)(2,1)S(1)}, bf16[2,1024,64]{2,1,0:T(8,128)(2,1)S(1)}, u32[]{:S(2)}, u32[]{:S(2)}) collective-permute-start(bf16[2,1024,64]{2,1,0:T(8,128)(2,1)S(1)} %bitcast.151), channel_id=1, source_target_pairs={{4,0},{6,2},{8,4},{10,6},{12,8},{14,10},{16,12},{18,14},{20,16},{2... | collective-permute-start | bytes 786440 | tf_op jit(solution)/shard_map/ppermute | solution.py:14
  110.2 79.3 %collective-permute-start.4 = (f32[2,1024,64]{1,2,0:T(8,128)S(1)}, f32[2,1024,64]{1,2,0:T(8,128)S(1)}, u32[]{:S(2)}, u32[]{:S(2)}) collective-permute-start(f32[2,1024,64]{1,2,0:T(8,128)S(1)} %get-tuple-element.272), channel_id=1, source_target_pairs={{0,2},{2,4},{4,6},{6,8},{8,10},{10,12},{12,14},{14,16},{16,18},{18... | collective-permute-start | bytes 1572872 | tf_op jit(solution)/shard_map/ppermute | solution.py:14
  116.6 79.0 %collective-permute-start.5 = (f32[2,1024,64]{1,2,0:T(8,128)S(1)}, f32[2,1024,64]{1,2,0:T(8,128)S(1)}, u32[]{:S(2)}, u32[]{:S(2)}) collective-permute-start(f32[2,1024,64]{1,2,0:T(8,128)S(1)} %get-tuple-element.273), channel_id=1, source_target_pairs={{0,4},{2,6},{4,8},{6,10},{8,12},{10,14},{12,16},{14,18},{16,20},{1... | collective-permute-start | bytes 1572872 | tf_op jit(solution)/shard_map/ppermute | solution.py:14
  197.7 249.4 %reduce-scatter.5.cloned.1.call-start = ((), (), s32[]{:S(2)}) async-start(), calls=%async_computation.3 | async-start | bytes 786432 | tf_op jit(solution)/shard_map/reduce_scatter | solution.py:101
  329.4 24.9 %collective-permute-start.6 = (bf16[2,1024,64]{2,1,0:T(8,128)(2,1)S(1)}, bf16[2,1024,64]{2,1,0:T(8,128)(2,1)S(1)}, u32[]{:S(2)}, u32[]{:S(2)}) collective-permute-start(bf16[2,1024,64]{2,1,0:T(8,128)(2,1)S(1)} %bitcast.153), channel_id=1, source_target_pairs={{2,0},{4,2},{6,4},{8,6},{10,8},{12,10},{14,12},{16,14},{18,16},{20... | collective-permute-start | bytes 786440 | tf_op jit(solution)/shard_map/ppermute | solution.py:14
  330.7 23.6 %collective-permute-start.7 = (bf16[2,1024,64]{2,1,0:T(8,128)(2,1)S(1)}, bf16[2,1024,64]{2,1,0:T(8,128)(2,1)S(1)}, u32[]{:S(2)}, u32[]{:S(2)}) collective-permute-start(bf16[2,1024,64]{2,1,0:T(8,128)(2,1)S(1)} %bitcast.154), channel_id=1, source_target_pairs={{4,0},{6,2},{8,4},{10,6},{12,8},{14,10},{16,12},{18,14},{20,16},{2... | collective-permute-start | bytes 786440 | tf_op jit(solution)/shard_map/ppermute | solution.py:14
  359.1 48.8 %collective-permute-start.8 = (f32[2,1024,64]{1,2,0:T(8,128)S(1)}, f32[2,1024,64]{1,2,0:T(8,128)S(1)}, u32[]{:S(2)}, u32[]{:S(2)}) collective-permute-start(f32[2,1024,64]{1,2,0:T(8,128)S(1)} %get-tuple-element.270), channel_id=1, source_target_pairs={{0,2},{2,4},{4,6},{6,8},{8,10},{10,12},{12,14},{14,16},{16,18},{18... | collective-permute-start | bytes 1572872 | tf_op jit(solution)/shard_map/ppermute | solution.py:14
  362.7 56.6 %collective-permute-start.9 = (f32[2,1024,64]{1,2,0:T(8,128)S(1)}, f32[2,1024,64]{1,2,0:T(8,128)S(1)}, u32[]{:S(2)}, u32[]{:S(2)}) collective-permute-start(f32[2,1024,64]{1,2,0:T(8,128)S(1)} %get-tuple-element.271), channel_id=1, source_target_pairs={{0,4},{2,6},{4,8},{6,10},{8,12},{10,14},{12,16},{14,18},{16,20},{1... | collective-permute-start | bytes 1572872 | tf_op jit(solution)/shard_map/ppermute | solution.py:14
Sparse Core Ops, SparseCore 0:
  197.8 36.2 reduce-scatter.2
  421.4 25.5 reduce-scatter.4
where the time goes:
time: 550 us; the launch traced here: 548 us
  waiting for transfers between devices  188 us (34%)
  blocking collectives  158 us (29%)
  starting transfers between devices  136 us (25%)
  other arithmetic  36.2 us (7%)
  between operations  14.3 us (3%)
  local copies, waits for them, and re-layouts  8.38 us (2%)
  matrix products  6.27 us (1%)
    psum x2, blocking collectives, orthonormal(): gram_matrix = lax.psum(gram_matrix, ('rows', 'cols')) / rows_total  155 us
    ppermute x10, starting transfers between devices, shifted(): lax.ppermute(value, axis, [(source, source + steps) for source in range(i...  136 us
    ppermute x10, waiting for transfers between devices, shifted(): lax.ppermute(value, axis, [(source, source + steps) for source in range(i...  126 us
    reduce_scatter x2, waiting for transfers between devices, affinity_pass(): return lax.psum_scatter(flattened, 'cols', scatter_dimension=0, tiled=True)  62.1 us
    another operation x6, other arithmetic, orthonormal(): lower_factor = jnp.linalg.cholesky(gram_matrix)  13 us
  transfers between devices with their start and end apart: 12, of which 6 were waited for; matrix products, arithmetic and copies ran while one was open for 0% of the time, Pallas kernels for 0%

commit v1 on v0

--- a/solution.py
+++ b/solution.py
@@ -2,6 +2,7 @@
 import jax.numpy as jnp
 from jax import lax
 from jax.sharding import PartitionSpec as P
+from jax.lax import psum
 
 BLK = 1024
 SHARPNESS = 6.0
@@ -53,7 +54,7 @@
         precision=lax.Precision.HIGHEST,
         preferred_element_type=jnp.float32,
     )
-    gram_matrix = lax.psum(gram_matrix, ("rows", "cols")) / rows_total
+    gram_matrix = psum(psum(gram_matrix, "cols"), "rows") / rows_total
     lower_factor = jnp.linalg.cholesky(gram_matrix)
     solved = lax.linalg.triangular_solve(
         lower_factor, sketch_rows, left_side=False, lower=True, transpose_a=True

time: 550 us -> 1760 us (3.20)
  the two profiles are of different devices: /device:TPU:1 before, /device:TPU:0 now
where the time goes in v1:
time: 1760 us; the launch traced here: 1750 us
  blocking collectives  1390 us (79%)
  waiting for transfers between devices  178 us (10%)
  matrix products  60.4 us (3%)
  other arithmetic  36.2 us (2%)
  starting transfers between devices  35 us (2%)
  local copies, waits for them, and re-layouts  26.9 us (2%)
    psum x4, blocking collectives, orthonormal(): gram_matrix = psum(psum(gram_matrix, 'cols'), 'rows') / rows_total  1390 us
    ppermute x10, waiting for transfers between devices, shifted(): lax.ppermute(value, axis, [(source, source + steps) for source in range(i...  127 us
    reduce_scatter x2, waiting for transfers between devices, affinity_pass(): return lax.psum_scatter(flattened, 'cols', scatter_dimension=0, tiled=True)  50.7 us
  transfers between devices with their start and end apart: 12, of which 7 were waited for; matrix products, arithmetic and copies ran while one was open for 0% of the time, Pallas kernels for 0%

profile of v1, /device:TPU:0, one launch (start us, length us, event | category | flops | bytes accessed | tf_op | source)
XLA Modules:
  0.0 1754.7 jit_solution(13738528905612419530)
XLA Ops:
  15.7 86.2 %collective-permute-done.2 = bf16[2,1024,64]{2,1,0:T(8,128)(2,1)S(1)} collective-permute-done((bf16[2,1024,64]{2,1,0:T(8,128)(2,1)S(1)}, bf16[2,1024,64]{2,1,0:T(8,128)(2,1)S(1)}, u32[]{:S(2)}, u32[]{:S(2)}) %collective-permute-start.2) | collective-permute-done | bytes 262176 | tf_op jit(solution)/shard_map/ppermute | solution.py:15
  103.4 3.8 pad_maximum_fusion
  108.5 44.5 %while.24 = (s32[]{:T(128)}, f32[6,1024,64]{1,2,0:T(8,128)}, s32[]{:T(128)}, s32[4,2]{0,1:T(2,128)S(1)}, s32[]{:T(128)}, /*index=5*/bf16[6,1024,384]{2,1,0:T(8,1...) while((s32[]{:T(128)}, f32[6,1024,64]{1,2,0:T(8,128)}, ...), condition=%wide.region_5.6_spmd, body=%wide.region_2.5_spmd.sunk | while | flops 1077018624 | bytes 10486193 | solution.py:95
  111.0 2.7 exponential_convert_fusion.4
  119.6 2.7 exponential_convert_fusion.4
  125.8 3.1 conditional.4
  131.4 2.7 exponential_convert_fusion.4
  137.5 3.2 conditional.4
  143.2 2.7 exponential_convert_fusion.4
  149.3 3.1 conditional.4
  155.7 23.2 %collective-permute-start.5 = (f32[2,1024,64]{1,2,0:T(8,128)S(1)}, f32[2,1024,64]{1,2,0:T(8,128)S(1)}, u32[]{:S(2)}, u32[]{:S(2)}) collective-permute-start(f32[2,1024,64]{1,2,0:T(8,128)S(1)} %get-tuple-element.273), channel_id=1, source_target_pairs={{0,4},{2,6},{4,8},{6,10},{8,12},{10,14},{12,16},{14,18},{16,20},{1... | collective-permute-start | bytes 1572872 | tf_op jit(solution)/shard_map/ppermute | solution.py:15
  178.9 6.7 collective-permute-done.5
  187.6 42.7 %reduce-scatter.3.cloned.1.call-done = f32[1024,64]{0,1:T(8,128)} async-done(((f32[2048,64]{0,1:T(8,128)}), f32[1024,64]{0,1:T(8,128)}) %reduce-scatter.3.cloned.1.call-update) | async-done | bytes 262160 | tf_op jit(solution)/shard_map/reduce_scatter | solution.py:102
  231.8 3.9 psum.28
  235.7 688.8 %psum.29 = f32[64,64]{0,1:T(8,128)S(1)} all-reduce(f32[64,64]{0,1:T(8,128)S(1)} %psum.28), channel_id=1, replica_groups=mesh['rows'=128,'cols'=2] {'rows'}, use_global_device_ids=true, to_apply=%region_8.9 | all-reduce | flops 4096 | bytes 32768 | tf_op jit(solution)/shard_map/psum | solution.py:57
  924.6 5.8 cholesky.44
  931.8 4.9 custom-call.6
  942.9 23.3 %collective-permute-done.6 = bf16[2,1024,64]{2,1,0:T(8,128)(2,1)S(1)} collective-permute-done((bf16[2,1024,64]{2,1,0:T(8,128)(2,1)S(1)}, bf16[2,1024,64]{2,1,0:T(8,128)(2,1)S(1)}, u32[]{:S(2)}, u32[]{:S(2)}) %collective-permute-start.6) | collective-permute-done | bytes 262176 | tf_op jit(solution)/shard_map/ppermute | solution.py:15
  969.1 44.5 %while.25 = (s32[]{:T(128)}, f32[6,1024,64]{1,2,0:T(8,128)}, s32[]{:T(128)}, s32[4,2]{0,1:T(2,128)S(1)}, s32[]{:T(128)}, /*index=5*/bf16[6,1024,384]{2,1,0:T(8,1...) while((s32[]{:T(128)}, f32[6,1024,64]{1,2,0:T(8,128)}, ...), condition=%wide.region_14.17_spmd, body=%wide.region_11.0_spmd.sunk | while | flops 1077018624 | bytes 10486193 | solution.py:95
  971.6 2.7 exponential_convert_fusion.5
  986.3 3.1 conditional.5
  991.9 2.7 exponential_convert_fusion.5
  998.0 3.2 conditional.5
  1003.7 2.7 exponential_convert_fusion.5
  1009.8 3.1 conditional.5
  1017.6 5.3 collective-permute-done.8
  1022.9 5.6 collective-permute-done.9
  1030.5 8.0 reduce-scatter.5.cloned.1.call-done
  1040.0 3.9 psum.30
  1043.8 689.0 %psum.31 = f32[64,64]{0,1:T(8,128)S(1)} all-reduce(f32[64,64]{0,1:T(8,128)S(1)} %psum.30), channel_id=1, replica_groups=mesh['rows'=128,'cols'=2] {'rows'}, use_global_device_ids=true, to_apply=%region_17.20 | all-reduce | flops 4096 | bytes 32768 | tf_op jit(solution)/shard_map/psum | solution.py:57
  1733.0 5.8 cholesky.55
  1740.2 4.9 custom-call.7
  (105 shorter events, 93.0 us)
Async XLA Ops:
  7.2 2.0 copy-start
  7.2 223.2 %reduce-scatter.3.cloned.1.call-start = ((), (), s32[]{:S(2)}) async-start(), calls=%async_computation.2 | async-start | bytes 786432 | tf_op jit(solution)/shard_map/reduce_scatter | solution.py:102
  9.1 3.0 copy-start.1
  9.2 5.9 copy-start.2
  9.5 93.8 %collective-permute-start = (bf16[2,1024,384]{2,1,0:T(8,128)(2,1)S(1)}, bf16[2,1024,384]{2,1,0:T(8,128)(2,1)}, u32[]{:S(2)}, u32[]{:S(2)}) collective-permute-start(bf16[2,1024,384]{2,1,0:T(8,128)(2,1)S(1)} %bitcast.145), channel_id=1, source_target_pairs={{2,0},{4,2},{6,4},{8,6},{10,8},{12,10},{14,12},{16,14},{18,16},{20... | collective-permute-start | bytes 4718600 | tf_op jit(solution)/shard_map/ppermute | solution.py:15
  10.8 92.5 %collective-permute-start.1 = (bf16[2,1024,384]{2,1,0:T(8,128)(2,1)S(1)}, bf16[2,1024,384]{2,1,0:T(8,128)(2,1)}, u32[]{:S(2)}, u32[]{:S(2)}) collective-permute-start(bf16[2,1024,384]{2,1,0:T(8,128)(2,1)S(1)} %bitcast.146), channel_id=1, source_target_pairs={{4,0},{6,2},{8,4},{10,6},{12,8},{14,10},{16,12},{18,14},{20,16},{2... | collective-permute-start | bytes 4718600 | tf_op jit(solution)/shard_map/ppermute | solution.py:15
  12.4 89.4 %collective-permute-start.2 = (bf16[2,1024,64]{2,1,0:T(8,128)(2,1)S(1)}, bf16[2,1024,64]{2,1,0:T(8,128)(2,1)S(1)}, u32[]{:S(2)}, u32[]{:S(2)}) collective-permute-start(bf16[2,1024,64]{2,1,0:T(8,128)(2,1)S(1)} %bitcast.150), channel_id=1, source_target_pairs={{2,0},{4,2},{6,4},{8,6},{10,8},{12,10},{14,12},{16,14},{18,16},{20... | collective-permute-start | bytes 786440 | tf_op jit(solution)/shard_map/ppermute | solution.py:15
  13.7 88.1 %collective-permute-start.3 = (bf16[2,1024,64]{2,1,0:T(8,128)(2,1)S(1)}, bf16[2,1024,64]{2,1,0:T(8,128)(2,1)S(1)}, u32[]{:S(2)}, u32[]{:S(2)}) collective-permute-start(bf16[2,1024,64]{2,1,0:T(8,128)(2,1)S(1)} %bitcast.151), channel_id=1, source_target_pairs={{4,0},{6,2},{8,4},{10,6},{12,8},{14,10},{16,12},{18,14},{20,16},{2... | collective-permute-start | bytes 786440 | tf_op jit(solution)/shard_map/ppermute | solution.py:15
  154.4 24.5 %collective-permute-start.4 = (f32[2,1024,64]{1,2,0:T(8,128)S(1)}, f32[2,1024,64]{1,2,0:T(8,128)S(1)}, u32[]{:S(2)}, u32[]{:S(2)}) collective-permute-start(f32[2,1024,64]{1,2,0:T(8,128)S(1)} %get-tuple-element.272), channel_id=1, source_target_pairs={{0,2},{2,4},{4,6},{6,8},{8,10},{10,12},{12,14},{14,16},{16,18},{18... | collective-permute-start | bytes 1572872 | tf_op jit(solution)/shard_map/ppermute | solution.py:15
  155.7 29.9 %collective-permute-start.5 = (f32[2,1024,64]{1,2,0:T(8,128)S(1)}, f32[2,1024,64]{1,2,0:T(8,128)S(1)}, u32[]{:S(2)}, u32[]{:S(2)}) collective-permute-start(f32[2,1024,64]{1,2,0:T(8,128)S(1)} %get-tuple-element.273), channel_id=1, source_target_pairs={{0,4},{2,6},{4,8},{6,10},{8,12},{10,14},{12,16},{14,18},{16,20},{1... | collective-permute-start | bytes 1572872 | tf_op jit(solution)/shard_map/ppermute | solution.py:15
  187.6 851.0 %reduce-scatter.5.cloned.1.call-start = ((), (), s32[]{:S(2)}) async-start(), calls=%async_computation.3 | async-start | bytes 786432 | tf_op jit(solution)/shard_map/reduce_scatter | solution.py:102
  940.3 25.9 %collective-permute-start.6 = (bf16[2,1024,64]{2,1,0:T(8,128)(2,1)S(1)}, bf16[2,1024,64]{2,1,0:T(8,128)(2,1)S(1)}, u32[]{:S(2)}, u32[]{:S(2)}) collective-permute-start(bf16[2,1024,64]{2,1,0:T(8,128)(2,1)S(1)} %bitcast.153), channel_id=1, source_target_pairs={{2,0},{4,2},{6,4},{8,6},{10,8},{12,10},{14,12},{16,14},{18,16},{20... | collective-permute-start | bytes 786440 | tf_op jit(solution)/shard_map/ppermute | solution.py:15
  941.6 24.6 %collective-permute-start.7 = (bf16[2,1024,64]{2,1,0:T(8,128)(2,1)S(1)}, bf16[2,1024,64]{2,1,0:T(8,128)(2,1)S(1)}, u32[]{:S(2)}, u32[]{:S(2)}) collective-permute-start(bf16[2,1024,64]{2,1,0:T(8,128)(2,1)S(1)} %bitcast.154), channel_id=1, source_target_pairs={{4,0},{6,2},{8,4},{10,6},{12,8},{14,10},{16,12},{18,14},{20,16},{2... | collective-permute-start | bytes 786440 | tf_op jit(solution)/shard_map/ppermute | solution.py:15
  1014.9 8.0 collective-permute-start.8
  1016.2 12.3 collective-permute-start.9
Sparse Core Ops, SparseCore 0:
  187.7 42.5 reduce-scatter.2
  1030.6 7.8 reduce-scatter.4
